TPU v7x, 256 devices: a whole 4x4x8 slice. The times are simulated.
256 devices in a mesh: pp: 2 (over x_hi), dp: 8 (over y, core), cp: 16 (over z, x_lo).
Axes of the slice: x: 4 (x_hi: 2, x_lo: 2; x = x_hi * 2 + x_lo), y: 4, z: 8, core: 2. Of those that a mesh axis runs over, the one named last changes fastest.
Arguments:
- tokens: bfloat16 [2, 2048, 3584], P('pp', 'cp'), may hold values from -6 to 6
- out_grad: bfloat16 [2, 2048, 3584], P('pp', 'cp'), may hold values from -6 to 6
- probs: bfloat16 [2, 2048, 8], P('pp', 'cp'), may hold values from 0.019897461 to 0.29882812
- expert_ids: int32 [2, 2048, 8], P('pp', 'cp'), may hold values from 0 to 15, all different within a row; in each aligned block of 128 rows (0 to 127, 128 to 255, ..., all dimensions but the last counted through in order) at most 80 rows name the same one
- w_gate: bfloat16 [2, 16, 1280, 3584], P('pp', 'cp', 'dp'), may hold values from -0.09375 to 0.09375
- w_up: bfloat16 [2, 16, 1280, 3584], P('pp', 'cp', 'dp'), may hold values from -0.09375 to 0.09375
- w_down: bfloat16 [2, 16, 1280, 3584], P('pp', 'cp', 'dp'), may hold values from -0.15625 to 0.15625
Outputs:
- passed_grad: bfloat16 [2, 2048, 3584], P('pp', 'cp', 'dp')
- prob_grad: float32 [2, 2048, 8], P('pp', 'cp')
- gate_grad: bfloat16 [2, 16, 1280, 3584], P('pp', 'cp', 'dp')
- up_grad: bfloat16 [2, 16, 1280, 3584], P('pp', 'cp', 'dp')
- down_grad: bfloat16 [2, 16, 1280, 3584], P('pp', 'cp', 'dp')
Inputs may be any that keep to these rules, and one draw needn't show every extreme that they name: `expert_ids`: in each aligned block of 128 tokens of a section, a token names 8 different experts, and no expert is named by more than 80 tokens of the block; some expert is named by exactly 80 tokens of some block.
All inputs are finite; a program needn't handle non-finite values.
Results may differ from a plain program's by a relative error of at most 0.012.
Values may be sent and summed in bfloat16 or wider, within the bound.
A program may use at most 128 MiB of HBM per device.

v0:
```python
import jax
import jax.numpy as jnp
from jax import lax
from jax.sharding import PartitionSpec as P

CAP_NUM, CAP_DEN = (5, 4)


def body(tokens, out_grad, probs, expert_ids, w_gate, w_up, w_down):
    tok_rows = tokens.shape[1]
    width = tokens.shape[2]
    top_count = probs.shape[2]
    experts = lax.axis_size("cp")
    replicas = lax.axis_size("dp")
    capacity = tok_rows * top_count * CAP_NUM // (CAP_DEN * experts)
    columns = width // replicas
    dp = lax.axis_index("dp")
    me = lax.axis_index("cp")
    own = lax.dynamic_slice_in_dim(jnp.stack([tokens[0], out_grad[0]]), dp * columns, columns, 2)
    blocks = lax.all_gather(own, "cp")
    ids_all = lax.all_gather(expert_ids[0], "cp")
    probs_all = lax.all_gather(probs[0], "cp")
    match = ids_all == me
    has = jnp.any(match, axis=2)
    prob_tok = jnp.sum(jnp.where(match, probs_all.astype(jnp.float32), 0.0), axis=2)
    has_i = has.astype(jnp.int32)
    slot = jnp.cumsum(has_i, axis=1) - has_i
    pick = (slot[:, None, :] == jnp.arange(capacity)[None, :, None]) & has[:, None, :]
    probs_in = jnp.sum(jnp.where(pick, prob_tok[:, None, :], 0.0), axis=2).reshape(-1, 1)
    rows = jnp.einsum(
        "bct,bstd->sbcd", pick.astype(jnp.bfloat16), blocks, preferred_element_type=jnp.float32
    ).astype(jnp.bfloat16)
    total_rows = experts * capacity
    rows = rows.reshape(2 * total_rows, columns)
    full = lax.all_gather(rows, "dp", axis=1, tiled=True)
    rows_in, grads_in = (full[:total_rows], full[total_rows:])
    gate_mat = w_gate[0, 0]
    up_mat = w_up[0, 0]
    down_mat = w_down[0, 0]
    by_feature = (((1,), (1,)), ((), ()))
    by_row = (((0,), (0,)), ((), ()))
    gate_pre = lax.dot_general(rows_in, gate_mat, by_feature, preferred_element_type=jnp.float32)
    up_pre = lax.dot_general(rows_in, up_mat, by_feature, preferred_element_type=jnp.float32)
    grad_proj = lax.dot_general(grads_in, down_mat, by_feature, preferred_element_type=jnp.float32)
    sigma = jax.nn.sigmoid(gate_pre)
    silu_gate = gate_pre * sigma
    hidden = (silu_gate * up_pre).astype(jnp.bfloat16)
    prob_part = jnp.sum(hidden.astype(jnp.float32) * grad_proj, axis=1)
    grad_hidden = probs_in * grad_proj
    grad_gate_pre = (grad_hidden * up_pre * sigma * (1.0 + gate_pre * (1.0 - sigma))).astype(
        jnp.bfloat16
    )
    grad_up_pre = (grad_hidden * silu_gate).astype(jnp.bfloat16)
    scaled_hidden = hidden
    scaled_grad = (probs_in * grads_in).astype(jnp.bfloat16)
    input_part = jnp.dot(grad_gate_pre, gate_mat, preferred_element_type=jnp.float32)
    input_part = (
        input_part + jnp.dot(grad_up_pre, up_mat, preferred_element_type=jnp.float32)
    ).astype(jnp.bfloat16)
    gate_grad = lax.dot_general(
        grad_gate_pre, rows_in, by_row, preferred_element_type=jnp.float32
    ).astype(jnp.bfloat16)
    up_grad = lax.dot_general(
        grad_up_pre, rows_in, by_row, preferred_element_type=jnp.float32
    ).astype(jnp.bfloat16)
    down_grad = lax.dot_general(
        scaled_hidden, scaled_grad, by_row, preferred_element_type=jnp.float32
    ).astype(jnp.bfloat16)
    reduced = lax.psum_scatter(input_part, "dp", scatter_dimension=1, tiled=True)
    back = lax.all_to_all(
        reduced.reshape(experts, capacity, columns), "cp", split_axis=0, concat_axis=0, tiled=True
    )
    back_probs = lax.all_to_all(
        prob_part.reshape(experts, capacity), "cp", split_axis=0, concat_axis=0, tiled=True
    )
    back_probs = lax.psum(back_probs, "dp")
    one_hot = expert_ids[0][:, :, None] == jnp.arange(experts)[None, None, :]
    has_e = jnp.any(one_hot, axis=1).astype(jnp.int32)
    slot_e = jnp.cumsum(has_e, axis=0) - has_e
    pick_e = (slot_e[:, :, None] == jnp.arange(capacity)[None, None, :]) & (has_e[:, :, None] > 0)
    input_sum = jnp.dot(
        pick_e.reshape(tok_rows, total_rows).astype(jnp.bfloat16),
        back.reshape(total_rows, columns),
        preferred_element_type=jnp.float32,
    )
    prob_te = jnp.sum(jnp.where(pick_e, back_probs[None], 0.0), axis=2)
    prob_grad = jnp.sum(jnp.where(one_hot, prob_te[:, None, :], 0.0), axis=2)
    passed = lax.ppermute(input_sum.astype(jnp.bfloat16), "pp", [(1, 0)])
    return (
        passed[None],
        prob_grad[None],
        gate_grad[None, None],
        up_grad[None, None],
        down_grad[None, None],
    )


def solution(mesh):
    in_specs = (
        P("pp", "cp", None),
        P("pp", "cp", None),
        P("pp", "cp", None),
        P("pp", "cp", None),
        P("pp", "cp", "dp", None),
        P("pp", "cp", "dp", None),
        P("pp", "cp", "dp", None),
    )
    out_specs = (
        P("pp", "cp", "dp"),
        P("pp", "cp", None),
        P("pp", "cp", "dp", None),
        P("pp", "cp", "dp", None),
        P("pp", "cp", "dp", None),
    )
    return jax.shard_map(body, mesh=mesh, in_specs=in_specs, out_specs=out_specs, check_vma=False)
```

profile of v0, /device:TPU:2, one launch (start us, length us, event | category | flops | bytes accessed | tf_op | source)
XLA Modules:
  0.0 369.4 jit_solution(6365457031545415939)
XLA Ops:
  7.2 0.0 copy-start
  7.2 0.0 copy-start.4
  7.2 0.0 copy-start.3
  7.2 0.0 all-gather.6.cloned.1.call-start
  7.3 1.6 copy.35
  8.9 1.6 copy.36
  10.5 0.7 fusion.45
  11.2 0.0 all-gather.6.cloned.1.call-update
  11.2 0.0 all-gather.4.cloned.1.call-start
  11.2 0.0 copy-done.4
  11.3 33.8 %all_gather.16 = bf16[16,128,8]{1,2,0:T(8,128)(2,1)S(1)} all-gather(bf16[1,128,8]{1,2,0:T(8,128)(2,1)S(1)} %copy-done.4), channel_id=1, replica_groups=mesh['pp'=2,'dp'=8,'cp'=16] {'cp'}, dimensions={0}, use_global_device_ids=true | all-gather | bytes 34816 | tf_op jit(solution)/shard_map/all_gather | solution.py:22
  45.1 0.0 copy-done.3
  45.1 33.9 %all_gather.15 = s32[16,128,8]{1,2,0:T(8,128)S(1)} all-gather(s32[1,128,8]{1,2,0:T(8,128)S(1)} %copy-done.3), channel_id=1, replica_groups=mesh['pp'=2,'dp'=8,'cp'=16] {'cp'}, dimensions={0}, use_global_device_ids=true | all-gather | bytes 69632 | tf_op jit(solution)/shard_map/all_gather | solution.py:21
  79.1 0.3 reduce_window_sum.23
  79.4 25.7 %all-gather.6.cloned.1.call-done = bf16[32,128,448]{1,2,0:T(8,128)(2,1)} async-done(((bf16[2,128,448]{1,2,0:T(8,128)(2,1)}), bf16[32,128,448]{1,2,0:T(8,128)(2,1)}) %all-gather.6.cloned.1.call-update) | async-done | bytes 3670032 | tf_op jit(solution)/shard_map/all_gather | solution.py:20
  105.0 3.7 convert_bitcast_fusion
  108.7 1.7 copy.37
  110.4 0.0 copy-start.2
  110.4 4.6 %copy.38 = bf16[2560,448]{0,1:T(8,128)(2,1)} copy(bf16[2560,448]{1,0:T(8,128)(2,1)} %bitcast.46) | data formatting | bytes 4587520 | tf_op jit(solution)/shard_map/reshape | solution.py:34
  115.0 0.0 all-gather.4.cloned.1.call-update
  115.0 0.2 reduce-scatter.2.cloned.1.call-start
  115.3 0.4 select_reduce_fusion.1
  115.6 0.1 mul.45
  115.7 94.2 %all-gather.4.cloned.1.call-done = bf16[2560,3584]{0,1:T(8,128)(2,1)} async-done(((bf16[2560,448]{0,1:T(8,128)(2,1)}), bf16[2560,3584]{0,1:T(8,128)(2,1)}) %all-gather.4.cloned.1.call-update) | async-done | bytes 18350096 | tf_op jit(solution)/shard_map/all_gather | solution.py:35
  209.9 0.0 copy-done.2
  209.9 0.0 copy-start.5
  210.0 5.4 %fusion.10 = f32[1280,160]{0,1:T(8,128)S(1)} fusion(bf16[2560,3584]{0,1:T(8,128)(2,1)} %all-gather.4.cloned.1.call-done, bf16[1,1,160,3584]{3,2,1,0:T(8,128)(2,1)S(1)} %copy-done.2), kind=kOutput, calls=%fused_computation.12 | convolution fusion | flops 1468006400 | bytes 11141120 | tf_op jit(solution)/shard_map/dot_general | solution.py:43
  215.4 0.0 copy-done
  215.4 0.0 copy-start.6
  215.4 6.1 %fusion.12 = f32[1280,160]{0,1:T(8,128)S(1)} fusion(bf16[2560,3584]{0,1:T(8,128)(2,1)} %all-gather.4.cloned.1.call-done, bf16[1,1,160,3584]{3,2,1,0:T(8,128)(2,1)S(1)} %copy-done), kind=kOutput, calls=%fused_computation.14 | convolution fusion | flops 1468006400 | bytes 11141120 | tf_op jit(solution)/shard_map/dot_general | solution.py:42
  221.4 0.0 copy-done.5
  221.5 0.4 copy-done.6
  221.9 3.2 multiply_reduce_fusion
  225.1 8.9 %fusion.29 = f32[1280,3584]{0,1:T(8,128)} fusion(bf16[1280,160]{0,1:T(8,128)(2,1)S(1)} %get-tuple-element.9, bf16[1,1,160,3584]{3,2,1,0:T(8,128)(2,1)S(1)} %copy-done), kind=kOutput, calls=%fused_computation.27 | convolution fusion | flops 1468006400 | bytes 19906560 | tf_op jit(solution)/shard_map/dot_general | solution.py:56
  234.0 12.3 %fusion = bf16[1280,3584]{0,1:T(8,128)(2,1)} fusion(f32[1280,3584]{0,1:T(8,128)} %fusion.29, bf16[1280,160]{0,1:T(8,128)(2,1)S(1)} %get-tuple-element.10, bf16[1,1,160,3584]{3,2,1,0:T(8,128)(2,1)S(1)} %copy-done.2), kind=kOutput, calls=%fused_computation.2 | convolution fusion | flops 1477181440 | bytes 29081600 | tf_op jit(solution)/shard_map/dot_general | solution.py:58
  246.3 0.0 reduce-scatter.2.cloned.1.call-update
  246.4 0.1 copy.32
  246.5 0.2 reduce_window_sum.22
  246.7 0.7 all_to_all.12
  247.4 8.5 %all-to-all-start.1 = ((f32[16,1,80]{2,1,0:T(1,128)}), f32[16,1,80]{2,1,0:T(1,128)S(1)}, u32[]{:S(2)}, u32[]{:S(2)}) async-start(f32[16,1,80]{2,1,0:T(1,128)} %all_to_all.12), calls=%async_computation.2 | async-start | bytes 16384 | tf_op jit(solution)/shard_map/all_to_all | solution.py:73
  255.9 0.1 copy.34
  255.9 0.1 copy.33
  256.0 49.9 %reduce-scatter.2.cloned.1.call-done = bf16[1280,448]{0,1:T(8,128)(2,1)} async-done(((bf16[1280,3584]{0,1:T(8,128)(2,1)}), bf16[1280,448]{0,1:T(8,128)(2,1)}) %reduce-scatter.2.cloned.1.call-update) | async-done | bytes 1146896 | tf_op jit(solution)/shard_map/reduce_scatter | solution.py:69
  306.0 2.4 copy.39
  308.4 0.0 all-to-all-done.1
  308.4 8.5 %all-to-all-start = ((bf16[16,80,448]{2,1,0:T(8,128)(2,1)}), bf16[16,80,448]{2,1,0:T(8,128)(2,1)S(1)}, u32[]{:S(2)}, u32[]{:S(2)}) async-start(bf16[16,80,448]{2,1,0:T(8,128)(2,1)} %bitcast.9), calls=%async_computation.1 | async-start | bytes 2621440 | tf_op jit(solution)/shard_map/all_to_all | solution.py:70
  316.9 7.8 %fusion.25 = bf16[1,1,160,3584]{3,2,1,0:T(8,128)(2,1)} fusion(bf16[1280,160]{0,1:T(8,128)(2,1)S(1)} %get-tuple-element.9, bf16[2560,3584]{0,1:T(8,128)(2,1)} %all-gather.4.cloned.1.call-done), kind=kOutput, calls=%fused_computation.21 | convolution fusion | flops 1468579840 | bytes 10731520 | tf_op jit(solution)/shard_map/dot_general | solution.py:60
  324.7 0.0 copy-start.7
  324.7 7.8 %fusion.22 = bf16[1,1,160,3584]{3,2,1,0:T(8,128)(2,1)} fusion(bf16[1280,160]{0,1:T(8,128)(2,1)S(1)} %get-tuple-element.10, bf16[2560,3584]{0,1:T(8,128)(2,1)} %all-gather.4.cloned.1.call-done), kind=kOutput, calls=%fused_computation.20 | convolution fusion | flops 1468579840 | bytes 10731520 | tf_op jit(solution)/shard_map/dot_general | solution.py:63
  332.5 0.0 copy-done.7
  332.5 0.0 copy-start.1
  332.5 7.9 %fusion.21 = bf16[1,1,160,3584]{3,2,1,0:T(8,128)(2,1)} fusion(bf16[1280,160]{0,1:T(8,128)(2,1)S(1)} %copy-done.7, f32[1280]{0:T(1024)S(1)} %mul.45, bf16[2560,3584]{0,1:T(8,128)(2,1)} %all-gather.4.cloned.1.call-done), kind=kOutput, calls=%fused_computation.19 | convolution fusion | flops 1482342400 | bytes 10736640 | tf_op jit(solution)/shard_map/dot_general | solution.py:66
  340.4 12.9 %psum.7 = f32[16,80]{1,0:T(8,128)S(1)} all-reduce(f32[16,80]{1,0:T(8,128)S(1)} %bitcast.51), channel_id=1, replica_groups=mesh['pp'=2,'dp'=8,'cp'=16] {'dp'}, use_global_device_ids=true, to_apply=%region_8.9 | all-reduce | flops 1280 | bytes 10240 | tf_op jit(solution)/shard_map/psum | solution.py:76
  353.4 0.0 all-to-all-done
  353.4 0.6 fusion.28
  354.0 1.3 collective-permute-start
  355.3 0.3 select_reduce_fusion
  355.6 0.6 select_reduce_fusion.2
  356.2 6.0 %collective-permute-done = bf16[128,448]{0,1:T(8,128)(2,1)S(1)} collective-permute-done((bf16[128,448]{0,1:T(8,128)(2,1)S(1)}, bf16[128,448]{0,1:T(8,128)(2,1)S(1)}, u32[]{:S(2)}, u32[]{:S(2)}) %collective-permute-start) | collective-permute-done | bytes 114720 | tf_op jit(solution)/shard_map/ppermute | solution.py:88
  362.2 0.6 copy.42
  362.9 0.0 copy-done.1
  (7 shorter events, 0.1 us)
Async XLA Ops:
  7.2 208.2 %copy-start = (bf16[1,1,160,3584]{3,2,1,0:T(8,128)(2,1)S(1)}, bf16[1,1,160,3584]{3,2,1,0:T(8,128)(2,1)}, u32[]{:S(2)}) copy-start(bf16[1,1,160,3584]{3,2,1,0:T(8,128)(2,1)} %param.11) | copy-start | bytes 3440644
  7.2 4.1 %copy-start.4 = (bf16[1,128,8]{1,2,0:T(8,128)(2,1)S(1)}, bf16[1,128,8]{1,2,0:T(8,128)(2,1)}, u32[]{:S(2)}) copy-start(bf16[1,128,8]{1,2,0:T(8,128)(2,1)} %param.9) | copy-start | bytes 6148
  7.2 37.9 %copy-start.3 = (s32[1,128,8]{1,2,0:T(8,128)S(1)}, s32[1,128,8]{1,2,0:T(8,128)}, u32[]{:S(2)}) copy-start(s32[1,128,8]{1,2,0:T(8,128)} %param.10) | copy-start | bytes 12292
  7.2 97.8 %all-gather.6.cloned.1.call-start = ((), (), s32[]{:S(2)}) async-start(), calls=%async_computation.5 | async-start | bytes 3899392 | tf_op jit(solution)/shard_map/all_gather | solution.py:20
  11.2 198.8 %all-gather.4.cloned.1.call-start = ((), (), s32[]{:S(2)}) async-start(), calls=%async_computation.3 | async-start | bytes 20643840 | tf_op jit(solution)/shard_map/all_gather | solution.py:35
  110.4 99.5 %copy-start.2 = (bf16[1,1,160,3584]{3,2,1,0:T(8,128)(2,1)S(1)}, bf16[1,1,160,3584]{3,2,1,0:T(8,128)(2,1)}, u32[]{:S(2)}) copy-start(bf16[1,1,160,3584]{3,2,1,0:T(8,128)(2,1)} %param.12) | copy-start | bytes 3440644
  115.0 190.9 %reduce-scatter.2.cloned.1.call-start = ((), (), s32[]{:S(2)}) async-start(), calls=%async_computation.4 | async-start | bytes 10321920 | tf_op jit(solution)/shard_map/reduce_scatter | solution.py:69
  209.9 11.5 %copy-start.5 = (bf16[2560,3584]{0,1:T(8,128)(2,1)S(1)}, bf16[2560,3584]{0,1:T(8,128)(2,1)}, u32[]{:S(2)}) copy-start(bf16[2560,3584]{0,1:T(8,128)(2,1)} %all-gather.4.cloned.1.call-done) | copy-start | bytes 55050244
  215.4 6.5 %copy-start.6 = (bf16[1,1,160,3584]{3,2,1,0:T(8,128)(2,1)S(1)}, bf16[1,1,160,3584]{3,2,1,0:T(8,128)(2,1)}, u32[]{:S(2)}) copy-start(bf16[1,1,160,3584]{3,2,1,0:T(8,128)(2,1)} %param.13) | copy-start | bytes 3440644
  247.4 61.0 %all-to-all-start.1 = ((f32[16,1,80]{2,1,0:T(1,128)}), f32[16,1,80]{2,1,0:T(1,128)S(1)}, u32[]{:S(2)}, u32[]{:S(2)}) async-start(f32[16,1,80]{2,1,0:T(1,128)} %all_to_all.12), calls=%async_computation.2 | async-start | bytes 16384 | tf_op jit(solution)/shard_map/all_to_all | solution.py:73
  308.4 45.0 %all-to-all-start = ((bf16[16,80,448]{2,1,0:T(8,128)(2,1)}), bf16[16,80,448]{2,1,0:T(8,128)(2,1)S(1)}, u32[]{:S(2)}, u32[]{:S(2)}) async-start(bf16[16,80,448]{2,1,0:T(8,128)(2,1)} %bitcast.9), calls=%async_computation.1 | async-start | bytes 2621440 | tf_op jit(solution)/shard_map/all_to_all | solution.py:70
  324.7 7.8 %copy-start.7 = (bf16[1280,160]{0,1:T(8,128)(2,1)S(1)}, bf16[1280,160]{0,1:T(8,128)(2,1)}, u32[]{:S(2)}) copy-start(bf16[1280,160]{0,1:T(8,128)(2,1)} %get-tuple-element.6) | copy-start | bytes 1228804
  332.5 30.3 %copy-start.1 = (bf16[1,1,160,3584]{3,2,1,0:T(8,128)(2,1)S(1)}, bf16[1,1,160,3584]{3,2,1,0:T(8,128)(2,1)}, u32[]{:S(2)}) copy-start(bf16[1,1,160,3584]{3,2,1,0:T(8,128)(2,1)} %param.11) | copy-start | bytes 3440644
  354.0 8.2 %collective-permute-start = (bf16[128,448]{0,1:T(8,128)(2,1)S(1)}, bf16[128,448]{0,1:T(8,128)(2,1)S(1)}, u32[]{:S(2)}, u32[]{:S(2)}) collective-permute-start(bf16[128,448]{0,1:T(8,128)(2,1)S(1)} %fusion.28), channel_id=1, source_target_pairs={{128,0},{129,1},{130,2},{131,3},{132,4},{133,5},{134,6},{135,7},{1... | collective-permute-start | bytes 344072 | tf_op jit(solution)/shard_map/ppermute | solution.py:88
Sparse Core Ops, SparseCore 0:
  11.3 93.6 all-gather.5
  115.1 94.7 all-gather.3
  246.5 59.4 reduce-scatter.1
where the time goes:
time: 370 us; the launch traced here: 369 us
  waiting for transfers between devices  176 us (48%)
  blocking collectives  80.7 us (22%)
  matrix products  63.8 us (17%)
  starting transfers between devices  18.6 us (5%)
  local copies, waits for them, and re-layouts  14 us (4%)
  between operations  13.9 us (4%)
    all_gather x1, waiting for transfers between devices, body(): full = lax.all_gather(rows, 'dp', axis=1, tiled=True)  94.2 us
    reduce_scatter x1, waiting for transfers between devices, body(): lax.psum_scatter(input_part, 'dp', scatter_dimension=1, tiled=True)  49.9 us
    all_gather x1, blocking collectives, body(): ids_all = lax.all_gather(expert_ids[0], 'cp')  33.9 us
    all_gather x1, blocking collectives, body(): probs_all = lax.all_gather(probs[0], 'cp')  33.8 us
    all_gather x1, waiting for transfers between devices, body(): blocks = lax.all_gather(own, 'cp')  25.7 us
    psum x1, blocking collectives, body(): back_probs = lax.psum(back_probs, 'dp')  12.9 us
    dot_general x1, matrix products, body(): jnp.dot(grad_up_pre, up_mat, preferred_element_type=jnp.float32)  12.3 us
    dot_general x1, matrix products, body(): jnp.dot(grad_gate_pre, gate_mat, preferred_element_type=jnp.float32)  8.93 us
  transfers between devices with their start and end apart: 6, of which 4 were waited for; matrix products, arithmetic and copies ran while one was open for 8% of the time, Pallas kernels for 0%

commit v1 on v0

--- a/solution.py
+++ b/solution.py
@@ -4,6 +4,9 @@
 from jax.sharding import PartitionSpec as P
 
 CAP_NUM, CAP_DEN = (5, 4)
+prepare_plate_up = lambda payload: jnp.concatenate(
+    lax.all_to_all(jnp.stack([payload] * lax.axis_size("dp"), 0), "dp", 0, 0), 1
+)
 
 
 def body(tokens, out_grad, probs, expert_ids, w_gate, w_up, w_down):
@@ -32,7 +35,7 @@
     ).astype(jnp.bfloat16)
     total_rows = experts * capacity
     rows = rows.reshape(2 * total_rows, columns)
-    full = lax.all_gather(rows, "dp", axis=1, tiled=True)
+    full = prepare_plate_up(rows)
     rows_in, grads_in = (full[:total_rows], full[total_rows:])
     gate_mat = w_gate[0, 0]
     up_mat = w_up[0, 0]

time: 370 us -> 484 us (1.31)
  waiting for transfers between devices: 176 us -> 281 us
  local copies, waits for them, and re-layouts: 14 us -> 29.4 us
  matrix products: 63.8 us -> 51.5 us
    all_to_all x0 -> x1, waiting for transfers between devices: none -> 201 us  [lax.all_to_all(jnp.stack([payload] * lax.axis_size('dp'), 0), 'dp', 0, 0)]
    all_gather x1 -> x0, waiting for transfers between devices: 94.2 us -> none  [body(): full = lax.all_gather(rows, 'dp', axis=1, tiled=True)]
    another operation x0 -> x2, local copies, waits for them, and re-layouts: none -> 9.61 us  [jnp.stack([payload] * lax.axis_size('dp'), 0)]
    slice x0 -> x1, local copies, waits for them, and re-layouts: none -> 7.82 us  [body(): rows_in, grads_in = (full[:total_rows], full[total_rows:])]
    all_to_all x0 -> x1, starting transfers between devices: none -> 5.86 us  [lax.all_to_all(jnp.stack([payload] * lax.axis_size('dp'), 0), 'dp', 0, 0)]
  transfers between devices with their start and end apart: 6 -> 6, of which waited for: 4 -> 4; matrix products, arithmetic and copies ran while one was open for 8% -> 5% of each run, Pallas kernels for 0% -> 0%
where the time goes in v1:
time: 484 us; the launch traced here: 483 us
  waiting for transfers between devices  281 us (58%)
  blocking collectives  81.2 us (17%)
  matrix products  51.5 us (11%)
  local copies, waits for them, and re-layouts  29.4 us (6%)
  starting transfers between devices  23.4 us (5%)
  between operations  14.3 us (3%)
    all_to_all x1, waiting for transfers between devices, lax.all_to_all(jnp.stack([payload] * lax.axis_size('dp'), 0), 'dp', 0, 0)  201 us
    reduce_scatter x1, waiting for transfers between devices, body(): lax.psum_scatter(input_part, 'dp', scatter_dimension=1, tiled=True)  48.5 us
    all_gather x1, blocking collectives, body(): ids_all = lax.all_gather(expert_ids[0], 'cp')  34.2 us
    all_gather x1, blocking collectives, body(): probs_all = lax.all_gather(probs[0], 'cp')  33.9 us
    all_gather x1, waiting for transfers between devices, body(): blocks = lax.all_gather(own, 'cp')  25.7 us
    psum x1, blocking collectives, body(): back_probs = lax.psum(back_probs, 'dp')  13.2 us
    dot_general x1, matrix products, body(): jnp.dot(grad_up_pre, up_mat, preferred_element_type=jnp.float32)  12.4 us
  transfers between devices with their start and end apart: 6, of which 4 were waited for; matrix products, arithmetic and copies ran while one was open for 5% of the time, Pallas kernels for 0%

profile of v1, /device:TPU:2, one launch (start us, length us, event | category | flops | bytes accessed | tf_op | source)
XLA Modules:
  0.0 483.3 jit_solution(610106559501658662)
XLA Ops:
  7.2 0.0 copy-start
  7.2 0.0 copy-start.6
  7.2 0.0 copy-start.5
  7.2 0.0 all-gather.3.cloned.1.call-start
  7.3 1.6 copy.36
  8.9 1.6 copy.37
  10.5 0.7 fusion.27
  11.2 0.0 all-gather.3.cloned.1.call-update
  11.2 0.0 copy-done.6
  11.2 33.9 %all_gather.13 = bf16[16,128,8]{1,2,0:T(8,128)(2,1)S(1)} all-gather(bf16[1,128,8]{1,2,0:T(8,128)(2,1)S(1)} %copy-done.6), channel_id=1, replica_groups=mesh['pp'=2,'dp'=8,'cp'=16] {'cp'}, dimensions={0}, use_global_device_ids=true | all-gather | bytes 34816 | tf_op jit(solution)/shard_map/all_gather | solution.py:25
  45.1 0.0 copy-done.5
  45.1 34.2 %all_gather.12 = s32[16,128,8]{1,2,0:T(8,128)S(1)} all-gather(s32[1,128,8]{1,2,0:T(8,128)S(1)} %copy-done.5), channel_id=1, replica_groups=mesh['pp'=2,'dp'=8,'cp'=16] {'cp'}, dimensions={0}, use_global_device_ids=true | all-gather | bytes 69632 | tf_op jit(solution)/shard_map/all_gather | solution.py:24
  79.3 0.3 reduce_window_sum.23
  79.6 25.7 %all-gather.3.cloned.1.call-done = bf16[32,128,448]{1,2,0:T(8,128)(2,1)} async-done(((bf16[2,128,448]{1,2,0:T(8,128)(2,1)}), bf16[32,128,448]{1,2,0:T(8,128)(2,1)}) %all-gather.3.cloned.1.call-update) | async-done | bytes 3670032 | tf_op jit(solution)/shard_map/all_gather | solution.py:23
  105.3 3.7 convert_bitcast_fusion
  109.0 1.7 copy.38
  110.7 3.1 copy.39
  113.9 6.5 %stack.7 = bf16[8,2560,448]{1,2,0:T(8,128)(2,1)} broadcast(bf16[2560,448]{0,1:T(8,128)(2,1)S(1)} %copy.39), dimensions={1,2} | broadcast | bytes 20643840 | tf_op jit(solution)/shard_map/stack | solution.py:8
  120.3 5.9 %all-to-all-start = ((bf16[8,2560,448]{1,2,0:T(8,128)(2,1)}), bf16[8,2560,448]{1,2,0:T(8,128)(2,1)}, u32[]{:S(2)}, u32[]{:S(2)}) async-start(bf16[8,2560,448]{1,2,0:T(8,128)(2,1)} %stack.7), calls=%async_computation | async-start | bytes 36700160 | tf_op jit(solution)/shard_map/all_to_all | solution.py:8
  126.2 0.2 reduce-scatter.2.cloned.1.call-start
  126.4 0.4 select_reduce_fusion.1
  126.8 0.1 mul.45
  126.9 200.7 %all-to-all-done = bf16[8,2560,448]{1,2,0:T(8,128)(2,1)} async-done(((bf16[8,2560,448]{1,2,0:T(8,128)(2,1)}), bf16[8,2560,448]{1,2,0:T(8,128)(2,1)}, u32[]{:S(2)}, u32[]{:S(2)}) %all-to-all-start) | async-done | bytes 18350112 | tf_op jit(solution)/shard_map/all_to_all | solution.py:8
  327.6 7.8 %fusion.29 = (bf16[1280,8,448]{0,2,1:T(8,128)(2,1)S(1)}, bf16[1280,8,448]{0,2,1:T(8,128)(2,1)S(1)}) fusion(bf16[2560,8,448]{0,2,1:T(8,128)(2,1)} %bitcast.6), kind=kLoop, calls=%fused_computation.51 | loop fusion | bytes 36700160 | tf_op jit(solution)/shard_map/slice | solution.py:39
  335.4 0.0 copy-start.2
  335.4 0.0 copy-start.3
  335.4 0.0 copy-done.4
  335.4 1.6 fusion.13
  337.1 1.9 copy-done.2
  339.0 0.0 copy-done
  339.0 1.6 fusion.10
  340.6 1.0 copy-done.3
  341.7 0.0 copy-done.7
  341.7 2.7 multiply_reduce_fusion
  344.3 8.9 %fusion.8 = f32[1280,3584]{0,1:T(8,128)} fusion(bf16[1280,160]{0,1:T(8,128)(2,1)S(1)} %get-tuple-element.11, bf16[1,1,160,3584]{3,2,1,0:T(8,128)(2,1)S(1)} %copy-done), kind=kOutput, calls=%fused_computation.16 | convolution fusion | flops 1468006400 | bytes 19906560 | tf_op jit(solution)/shard_map/dot_general | solution.py:59
  353.3 12.4 %fusion = bf16[1280,3584]{0,1:T(8,128)(2,1)} fusion(f32[1280,3584]{0,1:T(8,128)} %fusion.8, bf16[1280,160]{0,1:T(8,128)(2,1)S(1)} %get-tuple-element.12, bf16[1,1,160,3584]{3,2,1,0:T(8,128)(2,1)S(1)} %copy-done.4), kind=kOutput, calls=%fused_computation.2 | convolution fusion | flops 1477181440 | bytes 29081600 | tf_op jit(solution)/shard_map/dot_general | solution.py:61
  365.6 0.0 reduce-scatter.2.cloned.1.call-update
  365.7 0.7 all_to_all.16
  366.3 7.5 %all-to-all-start.2 = ((f32[16,1,80]{2,1,0:T(1,128)}), f32[16,1,80]{2,1,0:T(1,128)S(1)}, u32[]{:S(2)}, u32[]{:S(2)}) async-start(f32[16,1,80]{2,1,0:T(1,128)} %all_to_all.16), calls=%async_computation.3 | async-start | bytes 16384 | tf_op jit(solution)/shard_map/all_to_all | solution.py:76
  373.9 0.1 copy.33
  374.0 48.5 %reduce-scatter.2.cloned.1.call-done = bf16[1280,448]{0,1:T(8,128)(2,1)} async-done(((bf16[1280,3584]{0,1:T(8,128)(2,1)}), bf16[1280,448]{0,1:T(8,128)(2,1)}) %reduce-scatter.2.cloned.1.call-update) | async-done | bytes 1146896 | tf_op jit(solution)/shard_map/reduce_scatter | solution.py:72
  422.6 2.4 copy.40
  425.0 0.0 all-to-all-done.2
  425.0 8.5 %all-to-all-start.1 = ((bf16[16,80,448]{2,1,0:T(8,128)(2,1)}), bf16[16,80,448]{2,1,0:T(8,128)(2,1)S(1)}, u32[]{:S(2)}, u32[]{:S(2)}) async-start(bf16[16,80,448]{2,1,0:T(8,128)(2,1)} %bitcast.12), calls=%async_computation.2 | async-start | bytes 2621440 | tf_op jit(solution)/shard_map/all_to_all | solution.py:73
  433.5 0.1 copy.35
  433.6 0.2 reduce_window_sum.22
  433.8 0.1 copy.34
  433.8 7.9 %fusion.5 = bf16[1,1,160,3584]{3,2,1,0:T(8,128)(2,1)} fusion(bf16[1280,160]{0,1:T(8,128)(2,1)S(1)} %get-tuple-element.11, bf16[1280,3584]{0,1:T(8,128)(2,1)} %bitcast.56), kind=kOutput, calls=%fused_computation.9 | convolution fusion | flops 1468579840 | bytes 10731520 | tf_op jit(solution)/shard_map/dot_general | solution.py:63
  441.7 7.8 %fusion.6 = bf16[1,1,160,3584]{3,2,1,0:T(8,128)(2,1)} fusion(bf16[1280,160]{0,1:T(8,128)(2,1)S(1)} %get-tuple-element.12, bf16[1280,3584]{0,1:T(8,128)(2,1)} %bitcast.57), kind=kOutput, calls=%fused_computation.10 | convolution fusion | flops 1468579840 | bytes 10731520 | tf_op jit(solution)/shard_map/dot_general | solution.py:66
  449.5 0.0 slice-done
  449.5 0.0 slice-done.1
  449.5 0.0 slice-done.2
  449.5 0.0 copy-done.8
  449.6 0.0 copy-start.1
  449.6 4.2 fusion.4
  453.8 13.2 %psum.7 = f32[16,80]{1,0:T(8,128)S(1)} all-reduce(f32[16,80]{1,0:T(8,128)S(1)} %bitcast.67), channel_id=1, replica_groups=mesh['pp'=2,'dp'=8,'cp'=16] {'dp'}, use_global_device_ids=true, to_apply=%region_8.9 | all-reduce | flops 1280 | bytes 10240 | tf_op jit(solution)/shard_map/psum | solution.py:79
  467.0 0.0 all-to-all-done.1
  467.0 0.6 fusion.7
  467.7 1.3 collective-permute-start
  469.0 0.3 select_reduce_fusion
  469.3 0.6 select_reduce_fusion.2
  469.9 6.0 %collective-permute-done = bf16[128,448]{0,1:T(8,128)(2,1)S(1)} collective-permute-done((bf16[128,448]{0,1:T(8,128)(2,1)S(1)}, bf16[128,448]{0,1:T(8,128)(2,1)S(1)}, u32[]{:S(2)}, u32[]{:S(2)}) %collective-permute-start) | collective-permute-done | bytes 114720 | tf_op jit(solution)/shard_map/ppermute | solution.py:91
  475.8 0.6 copy.43
  476.5 0.0 copy-done.1
  (14 shorter events, 0.1 us)
Async XLA Ops:
  7.2 331.8 %copy-start = (bf16[1,1,160,3584]{3,2,1,0:T(8,128)(2,1)S(1)}, bf16[1,1,160,3584]{3,2,1,0:T(8,128)(2,1)}, u32[]{:S(2)}) copy-start(bf16[1,1,160,3584]{3,2,1,0:T(8,128)(2,1)} %param.11) | copy-start | bytes 3440644
  7.2 4.0 copy-start.6
  7.2 37.9 %copy-start.5 = (s32[1,128,8]{1,2,0:T(8,128)S(1)}, s32[1,128,8]{1,2,0:T(8,128)}, u32[]{:S(2)}) copy-start(s32[1,128,8]{1,2,0:T(8,128)} %param.10) | copy-start | bytes 12292
  7.2 98.1 %all-gather.3.cloned.1.call-start = ((), (), s32[]{:S(2)}) async-start(), calls=%async_computation.5 | async-start | bytes 3899392 | tf_op jit(solution)/shard_map/all_gather | solution.py:23
  120.3 207.2 %all-to-all-start = ((bf16[8,2560,448]{1,2,0:T(8,128)(2,1)}), bf16[8,2560,448]{1,2,0:T(8,128)(2,1)}, u32[]{:S(2)}, u32[]{:S(2)}) async-start(bf16[8,2560,448]{1,2,0:T(8,128)(2,1)} %stack.7), calls=%async_computation | async-start | bytes 36700160 | tf_op jit(solution)/shard_map/all_to_all | solution.py:8
  126.2 296.4 %reduce-scatter.2.cloned.1.call-start = ((), (), s32[]{:S(2)}) async-start(), calls=%async_computation.4 | async-start | bytes 10321920 | tf_op jit(solution)/shard_map/reduce_scatter | solution.py:72
  327.5 7.9 %copy-start.4 = (bf16[1,1,160,3584]{3,2,1,0:T(8,128)(2,1)S(1)}, bf16[1,1,160,3584]{3,2,1,0:T(8,128)(2,1)}, u32[]{:S(2)}) copy-start(bf16[1,1,160,3584]{3,2,1,0:T(8,128)(2,1)} %param.12) | copy-start | bytes 3440644
  335.4 3.6 copy-start.2
  335.4 6.3 %copy-start.3 = (bf16[1280,8,448]{0,2,1:T(8,128)(2,1)}, bf16[1280,8,448]{0,2,1:T(8,128)(2,1)S(1)}, u32[]{:S(2)}) copy-start(bf16[1280,8,448]{0,2,1:T(8,128)(2,1)S(1)} %get-tuple-element.9) | copy-start | bytes 27525124
  339.0 2.7 copy-start.7
  366.3 58.6 %all-to-all-start.2 = ((f32[16,1,80]{2,1,0:T(1,128)}), f32[16,1,80]{2,1,0:T(1,128)S(1)}, u32[]{:S(2)}, u32[]{:S(2)}) async-start(f32[16,1,80]{2,1,0:T(1,128)} %all_to_all.16), calls=%async_computation.3 | async-start | bytes 16384 | tf_op jit(solution)/shard_map/all_to_all | solution.py:76
  425.0 42.0 %all-to-all-start.1 = ((bf16[16,80,448]{2,1,0:T(8,128)(2,1)}), bf16[16,80,448]{2,1,0:T(8,128)(2,1)S(1)}, u32[]{:S(2)}, u32[]{:S(2)}) async-start(bf16[16,80,448]{2,1,0:T(8,128)(2,1)} %bitcast.12), calls=%async_computation.2 | async-start | bytes 2621440 | tf_op jit(solution)/shard_map/all_to_all | solution.py:73
  433.8 15.7 %slice-start = ((s8[9175040]{0:T(1024)(128)(4,1)}), s8[4194304]{0:T(1024)(128)(4,1)S(1)}, s32[]{:S(2)}) async-start(s8[9175040]{0:T(1024)(128)(4,1)} %bitcast.60), calls=%async_computation.6 | async-start | bytes 8388608
  433.8 15.7 %slice-start.1 = ((s8[9175040]{0:T(1024)(128)(4,1)}), s8[4194304]{0:T(1024)(128)(4,1)S(1)}, s32[]{:S(2)}) async-start(s8[9175040]{0:T(1024)(128)(4,1)} %bitcast.60), calls=%async_computation.7 | async-start | bytes 8388608
  441.7 7.8 %slice-start.2 = ((s8[9175040]{0:T(1024)(128)(4,1)}), s8[786432]{0:T(1024)(128)(4,1)S(1)}, s32[]{:S(2)}) async-start(s8[9175040]{0:T(1024)(128)(4,1)} %bitcast.60), calls=%async_computation.8 | async-start | bytes 1572864
  441.7 7.8 %copy-start.8 = (bf16[1280,160]{0,1:T(8,128)(2,1)S(1)}, bf16[1280,160]{0,1:T(8,128)(2,1)}, u32[]{:S(2)}) copy-start(bf16[1280,160]{0,1:T(8,128)(2,1)} %get-tuple-element.6) | copy-start | bytes 1228804
  449.6 26.9 %copy-start.1 = (bf16[1,1,160,3584]{3,2,1,0:T(8,128)(2,1)S(1)}, bf16[1,1,160,3584]{3,2,1,0:T(8,128)(2,1)}, u32[]{:S(2)}) copy-start(bf16[1,1,160,3584]{3,2,1,0:T(8,128)(2,1)} %param.11) | copy-start | bytes 3440644
  467.7 8.2 %collective-permute-start = (bf16[128,448]{0,1:T(8,128)(2,1)S(1)}, bf16[128,448]{0,1:T(8,128)(2,1)S(1)}, u32[]{:S(2)}, u32[]{:S(2)}) collective-permute-start(bf16[128,448]{0,1:T(8,128)(2,1)S(1)} %fusion.7), channel_id=1, source_target_pairs={{128,0},{129,1},{130,2},{131,3},{132,4},{133,5},{134,6},{135,7},{1... | collective-permute-start | bytes 344072 | tf_op jit(solution)/shard_map/ppermute | solution.py:91
Sparse Core Ops, SparseCore 0:
  11.3 93.9 all-gather.2
  365.8 56.7 reduce-scatter.1
